TPU v7x, 32 devices: a whole 2x2x4 slice. The times are simulated.
32 devices in a mesh: gy: 16 (over z, x, core), gx: 2 (over y).
Axes of the slice: x: 2, y: 2, z: 4, core: 2. Of those that a mesh axis runs over, the one named last changes fastest.
Arguments:
- level_set: float32 [1024, 1024], P('gy', 'gx'), may hold values from -6 to 6
- velocity: float32 [2, 1024, 1024], P(None, 'gy', 'gx'), may hold values from -2 to 2
- particles: float32 [2048, 3, 128], P(('gy', 'gx')), may hold values from -0.5 to 0.5
- escaped: int32 [2048, 128], P(('gy', 'gx')), may hold values 0 or 1
- home_cell: int32 [2048], P(('gy', 'gx')), may hold values from 0 to 32767
- land_cell: int32 [2048], P(('gy', 'gx')), may hold values from 0 to 32767
- dest_rank: int32 [2048], P(('gy', 'gx')), may hold values from 0 to 15, as said below
- block_count: int32 [32], P(('gy', 'gx')), may hold values from 48 to 64, as said below
Outputs:
- new_level: float32 [1024, 1024], P('gy', 'gx')
- moved_blocks: float32 [2048, 4, 128], P(('gy', 'gx'))
Inputs may be any that keep to these rules, and one draw needn't show every extreme that they name: `block_count`: live blocks are the first ones of a device; in every draw some device holds 64 live blocks. `dest_rank`: among one device's live blocks at most 4 go to one band; in every draw one band receives exactly 4 live blocks from every device.
All inputs are finite; a program needn't handle non-finite values. No bound on the sum of `escaped` on one device may be relied on, other than what follows from the above.
Results may differ from a plain program's by a relative error of at most 0.0003.
Values sent between devices are 32-bit elements; how exact they have to be, the bound alone decides.
A program may use at most 64 MiB of HBM per device.

v0:
```python
import jax
import jax.numpy as jnp
from jax import lax
from jax.sharding import PartitionSpec as P

CAP = 4


time_step = 0.3
epsilon_weno = 1e-06


def with_halo(cells, sides, width):
    for axis, dim in sides:
        count = lax.axis_size(axis)
        head = lax.slice_in_dim(cells, 0, width, axis=dim)
        tail = lax.slice_in_dim(cells, cells.shape[dim] - width, cells.shape[dim], axis=dim)
        cells = jnp.concatenate(
            [
                lax.ppermute(tail, axis, [(i, (i + 1) % count) for i in range(count)]),
                cells,
                lax.ppermute(head, axis, [((i + 1) % count, i) for i in range(count)]),
            ],
            axis=dim,
        )
    return cells


def shifted_2(block, axis, distance):
    devices = range(lax.axis_size(axis))
    route = [((i - distance) % len(devices), i) for i in devices]
    return lax.ppermute(block, axis, route)


def blended(a, b, c, d, e):
    smooth_one = 13.0 / 12.0 * (a - 2.0 * b + c) ** 2 + 0.25 * (a - 4.0 * b + 3.0 * c) ** 2
    smooth_two = 13.0 / 12.0 * (b - 2.0 * c + d) ** 2 + 0.25 * (b - d) ** 2
    smooth_three = 13.0 / 12.0 * (c - 2.0 * d + e) ** 2 + 0.25 * (3.0 * c - 4.0 * d + e) ** 2
    weight_one = 0.1 / (smooth_one + epsilon_weno) ** 2
    weight_two = 0.6 / (smooth_two + epsilon_weno) ** 2
    weight_three = 0.3 / (smooth_three + epsilon_weno) ** 2
    weight_sum = weight_one + weight_two + weight_three
    candidate = (
        weight_one * (a / 3.0 - 7.0 * b / 6.0 + 11.0 * c / 6.0)
        + weight_two * (-b / 6.0 + 5.0 * c / 6.0 + d / 3.0)
        + weight_three * (c / 3.0 + 5.0 * d / 6.0 - e / 6.0)
    )
    return candidate / weight_sum


def upwinded(shifted, advecting):
    differences = [shifted(k + 1) - shifted(k) for k in range(-3, 3)]
    left_sided = blended(
        differences[0], differences[1], differences[2], differences[3], differences[4]
    )
    right_sided = blended(
        differences[5], differences[4], differences[3], differences[2], differences[1]
    )
    return advecting * jnp.where(advecting > 0, left_sided, right_sided)


def tendency(padded, along_x, along_y):
    height = along_x.shape[0]
    across = along_x.shape[1]

    def columns(k):
        return padded[3 : 3 + height, 3 + k : 3 + k + across]

    def rows_at(k):
        return padded[3 + k : 3 + k + height, 3 : 3 + across]

    return -(upwinded(columns, along_x) + upwinded(rows_at, along_y))


def advect(offset_x, offset_y, corners):
    fraction_y = offset_y + 0.5
    fraction_x = offset_x + 0.5

    def mixture(component):
        c = corners[:, component]
        return (
            (1.0 - fraction_y) * (1.0 - fraction_x) * c[:, 0:1]
            + fraction_y * (1.0 - fraction_x) * c[:, 1:2]
            + (1.0 - fraction_y) * fraction_x * c[:, 2:3]
            + fraction_y * fraction_x * c[:, 3:4]
        )

    return (offset_x + time_step * mixture(0), offset_y + time_step * mixture(1))


def shards(level_set, velocity, particles, escaped, home_cell, land_cell, dest_rank, block_count):
    height, across = level_set.shape
    band_count = lax.axis_size("gy")
    slot_count = band_count * CAP
    block_total = particles.shape[0]
    per_block = particles.shape[2]
    stacked = jnp.concatenate([level_set[None], velocity], axis=0)
    extended = with_halo(stacked, (("gy", 1), ("gx", 2)), 9)
    surface = extended[0]
    flow_field = extended[1:]
    section_one = surface[3:-3, 3:-3] + time_step * tendency(
        surface, flow_field[0, 3:-3, 3:-3], flow_field[1, 3:-3, 3:-3]
    )
    section_two = 0.75 * surface[6:-6, 6:-6] + 0.25 * (
        section_one[3:-3, 3:-3]
        + time_step * tendency(section_one, flow_field[0, 6:-6, 6:-6], flow_field[1, 6:-6, 6:-6])
    )
    section_three = surface[9:-9, 9:-9] / 3.0 + 2.0 / 3.0 * (
        section_two[3:-3, 3:-3] + time_step * tendency(section_two, velocity[0], velocity[1])
    )
    corner_flow = flow_field[:, 9 : height + 10, 9 : across + 10]
    position = jnp.arange(block_total, dtype=jnp.int32)
    is_live = position < block_count[0]
    earlier_same = (
        (dest_rank[None, :] == dest_rank[:, None])
        & is_live[None, :]
        & (position[None, :] < position[:, None])
    )
    slot_rank = jnp.sum(earlier_same.astype(jnp.int32), axis=1)
    target = jnp.where(is_live, dest_rank * CAP + slot_rank, -1)
    chooser = jnp.arange(slot_count, dtype=jnp.int32)[:, None] == target[None, :]
    selector = chooser.astype(jnp.float32)
    cell_out = jnp.sum(jnp.where(chooser, land_cell[None, :], 0), axis=1).reshape(band_count, CAP)
    home_flat = home_cell // across * (across + 1) + home_cell % across
    flattened = corner_flow.reshape(2, -1)
    corners = jnp.stack(
        [
            flattened[:, home_flat],
            flattened[:, home_flat + across + 1],
            flattened[:, home_flat + 1],
            flattened[:, home_flat + across + 2],
        ],
        axis=-1,
    )
    corners = jnp.transpose(corners, (1, 0, 2))
    radius = particles[:, 2, :]
    weight = escaped.astype(jnp.float32) * radius
    new_x, new_y = advect(particles[:, 0, :], particles[:, 1, :], corners)
    payload = jnp.stack([new_x, new_y, radius, weight], axis=1).reshape(block_total, 4 * per_block)
    packed = jnp.dot(selector, payload, precision=lax.Precision.HIGHEST).reshape(
        band_count, CAP, 4 * per_block
    )
    arrived, cells_in = (
        lax.all_to_all(packed, "gy", split_axis=0, concat_axis=0, tiled=True),
        lax.all_to_all(cell_out, "gy", split_axis=0, concat_axis=0, tiled=True),
    )
    moved_rows = arrived.reshape(slot_count, 4, per_block)
    cells_in = cells_in.reshape(slot_count)
    fraction_y = moved_rows[:, 1, :] + 0.5
    fraction_x = moved_rows[:, 0, :] + 0.5
    carried = moved_rows[:, 3, :]
    low_low = jnp.sum(carried * (1.0 - fraction_y) * (1.0 - fraction_x), axis=1)
    high_low = jnp.sum(carried * fraction_y * (1.0 - fraction_x), axis=1)
    low_high = jnp.sum(carried * (1.0 - fraction_y) * fraction_x, axis=1)
    high_high = jnp.sum(carried * fraction_y * fraction_x, axis=1)
    anchor = cells_in // across * (across + 1) + cells_in % across
    deposit = jnp.zeros(((height + 1) * (across + 1),), jnp.float32)
    deposit = deposit.at[anchor].add(low_low)
    deposit = deposit.at[anchor + across + 1].add(high_low)
    deposit = deposit.at[anchor + 1].add(low_high)
    deposit = deposit.at[anchor + across + 2].add(high_high)
    deposit = deposit.reshape(height + 1, across + 1)
    incoming = shifted_2(deposit[height], "gy", 1)
    deposit = deposit.at[0].add(incoming)
    sideways = shifted_2(deposit[:height, across], "gx", 1)
    correction = deposit[:height, :across].at[:, 0].add(sideways)
    return (section_three + correction, moved_rows)


def solution(mesh):
    in_specs = (
        P("gy", "gx"),
        P(None, "gy", "gx"),
        P(("gy", "gx"), None, None),
        P(("gy", "gx"), None),
        P(("gy", "gx")),
        P(("gy", "gx")),
        P(("gy", "gx")),
        P(("gy", "gx")),
    )
    out_specs = (P("gy", "gx"), P(("gy", "gx"), None, None))
    return jax.shard_map(shards, mesh=mesh, in_specs=in_specs, out_specs=out_specs, check_vma=False)
```

profile of v0, /device:TPU:0, one launch (start us, length us, event | category | flops | bytes accessed | tf_op | source)
XLA Modules:
  0.0 95.5 jit_solution(13410484799370685124)
XLA Ops:
  0.7 1.0 %pad_maximum_fusion.11 = (f32[3,9,512]{2,1,0:T(8,128)S(1)}, f32[3,9,512]{2,1,0:T(8,128)S(1)}) fusion(f32[2,64,512]{2,1,0:T(8,128)} %param.13, f32[1,64,512]{2,1,0:T(8,128)} %bitcast.110), kind=kLoop, calls=%fused_computation.69 | loop fusion | flops 27648 | bytes 503808 | tf_op jit(solution)/shard_map/slice | solution.py:17
  1.6 0.5 collective-permute-start
  2.2 5.0 %collective-permute-start.1 = (f32[3,9,512]{2,1,0:T(8,128)S(1)}, f32[3,9,512]{2,1,0:T(8,128)S(1)}, u32[]{:S(2)}, u32[]{:S(2)}) collective-permute-start(f32[3,9,512]{2,1,0:T(8,128)S(1)} %get-tuple-element.39), channel_id=1, source_target_pairs={{2,0},{4,2},{6,4},{8,6},{10,8},{12,10},{14,12},{16,14},{18,16},{20... | collective-permute-start | bytes 165896 | tf_op jit(solution)/shard_map/ppermute | solution.py:22
  7.9 0.9 convert_reduce_fusion
  8.8 0.7 add_select_fusion.1
  9.4 0.8 select_reduce_fusion
  10.2 0.7 all_to_all.9
  10.9 3.6 %all-to-all-start = ((s32[16,1,4]{2,1,0:T(1,128)}), s32[16,1,4]{2,1,0:T(1,128)S(1)}, u32[]{:S(2)}, u32[]{:S(2)}) async-start(s32[16,1,4]{2,1,0:T(1,128)} %bitcast.9), calls=%async_computation | async-start | bytes 16384 | tf_op jit(solution)/shard_map/all_to_all | solution.py:145
  14.5 0.7 compare_select_fusion.6
  15.3 0.8 fusion.23
  16.1 0.6 compare_reduce_fusion
  16.7 4.2 %all-to-all-done = s32[16,1,4]{2,1,0:T(1,128)S(1)} async-done(((s32[16,1,4]{2,1,0:T(1,128)}), s32[16,1,4]{2,1,0:T(1,128)S(1)}, u32[]{:S(2)}, u32[]{:S(2)}) %all-to-all-start) | async-done | bytes 288 | tf_op jit(solution)/shard_map/all_to_all | solution.py:145
  20.9 0.5 broadcast.853
  21.4 0.7 reduce.15
  22.1 0.1 reshape.352
  22.2 1.0 %pad_maximum_fusion.8 = (f32[3,82,9]{2,1,0:T(8,128)S(1)}, f32[3,82,9]{2,1,0:T(8,128)S(1)}) fusion(f32[3,9,512]{2,1,0:T(8,128)S(1)} %collective-permute-done.1, f32[3,9,512]{2,1,0:T(8,128)S(1)} %collective-permute-done, f32[2,64,512]{2,1,0:T(8,128)} %param.13, f32[1,64,512]{2,1,0:T(8,128)} %bitcast.111), kind=kLoop, calls=%fused_computation.44 | loop fusion | flops 13284 | bytes 521520 | tf_op jit(solution)/shard_map/slice | solution.py:17
  23.2 1.8 %collective-permute-start.3 = (f32[3,82,9]{2,1,0:T(8,128)S(1)}, f32[3,82,9]{2,1,0:T(8,128)S(1)}, u32[]{:S(2)}, u32[]{:S(2)}) collective-permute-start(f32[3,82,9]{2,1,0:T(8,128)S(1)} %get-tuple-element.37), channel_id=1, source_target_pairs={{1,0},{0,1},{3,2},{2,3},{5,4},{4,5},{7,6},{6,7},{9,8},{8,9},{11,10... | collective-permute-start | bytes 26576 | tf_op jit(solution)/shard_map/ppermute | solution.py:22
  25.0 0.3 collective-permute-start.2
  25.3 4.4 %collective-permute-done.3 = f32[3,82,9]{2,1,0:T(8,128)S(1)} collective-permute-done((f32[3,82,9]{2,1,0:T(8,128)S(1)}, f32[3,82,9]{2,1,0:T(8,128)S(1)}, u32[]{:S(2)}, u32[]{:S(2)}) %collective-permute-start.3) | collective-permute-done | bytes 8888 | tf_op jit(solution)/shard_map/ppermute | solution.py:22
  29.7 1.0 %pad_maximum_fusion.1 = f32[2,65,513]{2,1,0:T(8,128)S(1)} fusion(f32[3,82,9]{2,1,0:T(8,128)S(1)} %collective-permute-done.3, f32[3,9,512]{2,1,0:T(8,128)S(1)} %collective-permute-done.1, f32[3,9,512]{2,1,0:T(8,128)S(1)} %collective-permute-done, f32[2,64,512]{2,1,0:T(8,128)} %param.13, f32[1,64,512]{2,1,0:T(8,128)} %bitcast.112), kind=kLoop, calls=%fused_computation.9 | loop fusion | flops 266760 | bytes 779424 | tf_op jit(solution)/shard_map/concatenate | solution.py:18
  30.7 0.4 reshape.353
  31.2 8.4 %copy.68 = f32[2,33345]{0,1:T(8,128)} copy(f32[2,33345]{1,0:T(2,128)S(1)} %reshape.353) | data formatting | bytes 533520 | tf_op jit(solution)/shard_map/reshape | solution.py:125
  39.6 6.5 %gather_fusion.2 = f32[64,2]{1,0:T(8,128)S(1)} fusion(f32[2,33345]{0,1:T(8,128)} %copy.68, s32[1024]{0:T(1024)S(1)} %get-tuple-element.63), kind=kCustom, calls=%fused_computation.2 | custom fusion | bytes 1280 | tf_op jit(solution)/shard_map/gather | solution.py:130
  46.1 6.5 %gather_fusion.3 = f32[64,2]{1,0:T(8,128)S(1)} fusion(f32[2,33345]{0,1:T(8,128)} %copy.68, s32[1024]{0:T(1024)S(1)} %get-tuple-element.62), kind=kCustom, calls=%fused_computation.3 | custom fusion | bytes 1280 | tf_op jit(solution)/shard_map/gather | solution.py:131
  52.7 6.5 %gather_fusion.1 = f32[64,2]{1,0:T(8,128)S(1)} fusion(f32[2,33345]{0,1:T(8,128)} %copy.68, s32[1024]{0:T(1024)S(1)} %pad_clamp_fusion.2), kind=kCustom, calls=%fused_computation.1 | custom fusion | bytes 1280 | tf_op jit(solution)/shard_map/gather | solution.py:129
  59.2 6.5 %gather_fusion = f32[64,2]{1,0:T(8,128)S(1)} fusion(f32[2,33345]{0,1:T(8,128)} %copy.68, s32[1024]{0:T(1024)S(1)} %pad_clamp_fusion.3), kind=kCustom, calls=%fused_computation | custom fusion | bytes 1280 | tf_op jit(solution)/shard_map/gather | solution.py:128
  65.8 0.1 multiply_add_fusion.2
  66.0 0.1 copy.76
  66.1 0.3 fusion.25
  66.4 0.7 copy.77
  67.1 3.5 %all-to-all-start.1 = ((f32[16,4,512]{2,1,0:T(4,128)}), f32[16,4,512]{2,1,0:T(4,128)S(1)}, u32[]{:S(2)}, u32[]{:S(2)}) async-start(f32[16,4,512]{2,1,0:T(4,128)} %copy.77), calls=%async_computation.1 | async-start | bytes 262144 | tf_op jit(solution)/shard_map/all_to_all | solution.py:144
  70.7 0.3 pad_maximum_fusion
  71.0 7.5 %all-to-all-done.1 = f32[16,4,512]{2,1,0:T(4,128)S(1)} async-done(((f32[16,4,512]{2,1,0:T(4,128)}), f32[16,4,512]{2,1,0:T(4,128)S(1)}, u32[]{:S(2)}, u32[]{:S(2)}) %all-to-all-start.1) | async-done | bytes 131104 | tf_op jit(solution)/shard_map/all_to_all | solution.py:144
  78.7 0.1 multiply_reduce_fusion
  78.8 0.9 scatter_custom_fusion
  79.8 0.9 scatter_fusion
  80.7 0.9 scatter_fusion.1
  81.7 0.9 scatter_fusion.2
  82.7 2.2 %multiply_add_fusion = f32[76,524]{1,0:T(8,128)S(1)} fusion(f32[82,530]{1,0:T(8,128)S(1)} %slice_bitcast_fusion, f32[3,82,530]{2,1,0:T(8,128)S(1)} %pad_maximum_fusion), kind=kLoop, calls=%fused_computation.20 | loop fusion | flops 10752480 | bytes 2548736 | tf_op jit(solution)/shard_map/add | solution.py:101
  84.9 0.2 reshape.356
  85.1 3.3 %collective-permute-done.4 = f32[513]{0:T(1024)S(1)} collective-permute-done((f32[513]{0:T(1024)S(1)}, f32[513]{0:T(1024)S(1)}, u32[]{:S(2)}, u32[]{:S(2)}) %collective-permute-start.4) | collective-permute-done | bytes 2084 | tf_op jit(solution)/shard_map/ppermute | solution.py:32
  88.5 0.1 slice_reduce_fusion
  88.6 1.8 %collective-permute-start.5 = (f32[64]{0:T(128)S(1)}, f32[64]{0:T(128)S(1)}, u32[]{:S(2)}, u32[]{:S(2)}) collective-permute-start(f32[64]{0:T(128)S(1)} %slice_reduce_fusion), channel_id=1, source_target_pairs={{1,0},{0,1},{3,2},{2,3},{5,4},{4,5},{7,6},{6,7},{9,8},{8,9},{11,10... | collective-permute-start | bytes 776 | tf_op jit(solution)/shard_map/ppermute | solution.py:32
  90.4 2.0 %fusion.4 = f32[70,518]{1,0:T(8,128)S(1)} fusion(f32[82,530]{1,0:T(8,128)S(1)} %slice_bitcast_fusion, f32[76,524]{1,0:T(8,128)S(1)} %multiply_add_fusion, f32[3,82,530]{2,1,0:T(8,128)S(1)} %pad_maximum_fusion), kind=kLoop, calls=%fused_computation.34 | loop fusion | flops 9898980 | bytes 2465680 | tf_op jit(solution)/shard_map/add | solution.py:104
  92.5 0.1 copy.81
  92.6 0.7 add_select_fusion
  93.2 0.2 scatter-add.43
  93.4 2.1 %fusion.10 = f32[64,512]{1,0:T(8,128)} fusion(f32[64,512]{1,0:T(8,128)S(1)} %scatter-add.43, f32[82,530]{1,0:T(8,128)S(1)} %slice_bitcast_fusion, f32[70,518]{1,0:T(8,128)S(1)} %fusion.4, f32[2,64,512]{2,1,0:T(8,128)S(1)} %copy-done), kind=kLoop, calls=%fused_computation.51 | loop fusion | flops 8978432 | bytes 2359296 | tf_op jit(solution)/shard_map/add | solution.py:167
  (40 shorter events, 0.8 us)
Async XLA Ops:
  0.6 70.0 %copy-start.1 = (f32[64,512]{1,0:T(8,128)S(1)}, f32[64,512]{1,0:T(8,128)}, u32[]{:S(2)}) copy-start(f32[64,512]{1,0:T(8,128)} %param.12) | copy-start | bytes 393220
  0.6 70.0 %copy-start = (f32[2,64,512]{2,1,0:T(8,128)S(1)}, f32[2,64,512]{2,1,0:T(8,128)}, u32[]{:S(2)}) copy-start(f32[2,64,512]{2,1,0:T(8,128)} %param.13) | copy-start | bytes 786436
  0.7 65.1 %copy-start.3 = (f32[64,3,128]{2,0,1:T(8,128)S(1)}, f32[64,3,128]{2,0,1:T(8,128)}, u32[]{:S(2)}) copy-start(f32[64,3,128]{2,0,1:T(8,128)} %param.14) | copy-start | bytes 294916
  1.6 20.6 %collective-permute-start = (f32[3,9,512]{2,1,0:T(8,128)S(1)}, f32[3,9,512]{2,1,0:T(8,128)S(1)}, u32[]{:S(2)}, u32[]{:S(2)}) collective-permute-start(f32[3,9,512]{2,1,0:T(8,128)S(1)} %get-tuple-element.38), channel_id=1, source_target_pairs={{0,2},{2,4},{4,6},{6,8},{8,10},{10,12},{12,14},{14,16},{16,18},{18... | collective-permute-start | bytes 165896 | tf_op jit(solution)/shard_map/ppermute | solution.py:20
  2.2 20.0 %collective-permute-start.1 = (f32[3,9,512]{2,1,0:T(8,128)S(1)}, f32[3,9,512]{2,1,0:T(8,128)S(1)}, u32[]{:S(2)}, u32[]{:S(2)}) collective-permute-start(f32[3,9,512]{2,1,0:T(8,128)S(1)} %get-tuple-element.39), channel_id=1, source_target_pairs={{2,0},{4,2},{6,4},{8,6},{10,8},{12,10},{14,12},{16,14},{18,16},{20... | collective-permute-start | bytes 165896 | tf_op jit(solution)/shard_map/ppermute | solution.py:22
  10.9 10.0 %all-to-all-start = ((s32[16,1,4]{2,1,0:T(1,128)}), s32[16,1,4]{2,1,0:T(1,128)S(1)}, u32[]{:S(2)}, u32[]{:S(2)}) async-start(s32[16,1,4]{2,1,0:T(1,128)} %bitcast.9), calls=%async_computation | async-start | bytes 16384 | tf_op jit(solution)/shard_map/all_to_all | solution.py:145
  23.2 6.5 %collective-permute-start.3 = (f32[3,82,9]{2,1,0:T(8,128)S(1)}, f32[3,82,9]{2,1,0:T(8,128)S(1)}, u32[]{:S(2)}, u32[]{:S(2)}) collective-permute-start(f32[3,82,9]{2,1,0:T(8,128)S(1)} %get-tuple-element.37), channel_id=1, source_target_pairs={{1,0},{0,1},{3,2},{2,3},{5,4},{4,5},{7,6},{6,7},{9,8},{8,9},{11,10... | collective-permute-start | bytes 26576 | tf_op jit(solution)/shard_map/ppermute | solution.py:22
  25.0 45.6 %collective-permute-start.2 = (f32[3,82,9]{2,1,0:T(8,128)S(1)}, f32[3,82,9]{2,1,0:T(8,128)S(1)}, u32[]{:S(2)}, u32[]{:S(2)}) collective-permute-start(f32[3,82,9]{2,1,0:T(8,128)S(1)} %get-tuple-element.36), channel_id=1, source_target_pairs={{0,1},{1,0},{2,3},{3,2},{4,5},{5,4},{6,7},{7,6},{8,9},{9,8},{10,11... | collective-permute-start | bytes 26576 | tf_op jit(solution)/shard_map/ppermute | solution.py:20
  67.1 11.4 %all-to-all-start.1 = ((f32[16,4,512]{2,1,0:T(4,128)}), f32[16,4,512]{2,1,0:T(4,128)S(1)}, u32[]{:S(2)}, u32[]{:S(2)}) async-start(f32[16,4,512]{2,1,0:T(4,128)} %copy.77), calls=%async_computation.1 | async-start | bytes 262144 | tf_op jit(solution)/shard_map/all_to_all | solution.py:144
  78.6 16.9 %copy-start.2 = (f32[64,4,128]{2,1,0:T(4,128)}, f32[64,4,128]{2,1,0:T(4,128)S(1)}, u32[]{:S(2)}) copy-start(f32[64,4,128]{2,1,0:T(4,128)S(1)} %reshape.355) | copy-start | bytes 393220
  82.7 5.7 %collective-permute-start.4 = (f32[513]{0:T(1024)S(1)}, f32[513]{0:T(1024)S(1)}, u32[]{:S(2)}, u32[]{:S(2)}) collective-permute-start(f32[513]{0:T(1024)S(1)} %slice.454), channel_id=1, source_target_pairs={{30,0},{0,2},{2,4},{4,6},{6,8},{8,10},{10,12},{12,14},{14,16},{16,... | collective-permute-start | bytes 6164 | tf_op jit(solution)/shard_map/ppermute | solution.py:32
  88.6 3.9 %collective-permute-start.5 = (f32[64]{0:T(128)S(1)}, f32[64]{0:T(128)S(1)}, u32[]{:S(2)}, u32[]{:S(2)}) collective-permute-start(f32[64]{0:T(128)S(1)} %slice_reduce_fusion), channel_id=1, source_target_pairs={{1,0},{0,1},{3,2},{2,3},{5,4},{4,5},{7,6},{6,7},{9,8},{8,9},{11,10... | collective-permute-start | bytes 776 | tf_op jit(solution)/shard_map/ppermute | solution.py:32
where the time goes:
time: 96.1 us; the launch traced here: 95.5 us
  local copies, waits for them, and re-layouts  38 us (40%)
  other arithmetic  19.5 us (20%)
  waiting for transfers between devices  19.4 us (20%)
  starting transfers between devices  16.6 us (17%)
  between operations  1.66 us (2%)
    reshape x2, local copies, waits for them, and re-layouts, shards(): flattened = corner_flow.reshape(2, -1)  8.87 us
    all_to_all x1, waiting for transfers between devices, shards(): lax.all_to_all(packed, 'gy', split_axis=0, concat_axis=0, tiled=True)  7.49 us
    ppermute x2, starting transfers between devices, with_halo(): lax.ppermute(head, axis, [((i + 1) % count, i) for i in range(count)])  6.82 us
    gather x2, local copies, waits for them, and re-layouts, shards(): flattened[:, home_flat + across + 1]  6.53 us
    gather x2, local copies, waits for them, and re-layouts, shards(): flattened[:, home_flat + across + 2]  6.53 us
    gather x2, local copies, waits for them, and re-layouts, shards(): flattened[:, home_flat]  6.53 us
    gather x2, local copies, waits for them, and re-layouts, shards(): flattened[:, home_flat + 1]  6.52 us
    ppermute x2, waiting for transfers between devices, with_halo(): lax.ppermute(head, axis, [((i + 1) % count, i) for i in range(count)])  4.43 us
  transfers between devices with their start and end apart: 8, of which 4 were waited for; matrix products, arithmetic and copies ran while one was open for 50% of the time, Pallas kernels for 0%

commit v1 on v0

v1 whole, which is shorter than its diff:
```python
import functools

import jax
import jax.numpy as jnp
from jax import lax
from jax.experimental import pallas as pl
from jax.experimental.pallas import tpu as pltpu
from jax.sharding import PartitionSpec as P

CAP = 4
FIELDS = 4
STEP = 0.3
EPS4 = 4e-06
LANES = 128
DEEP = 16
THIN = 8
MESH = pl.DeviceIdType.MESH
EXACT = lax.Precision.HIGHEST


def one_sided(speed, lower, upper, s_m2, s_m1, s_0, s_p1, s_p2):
    ahead = speed > 0
    c = jnp.where(ahead, lower, upper)
    p = jnp.where(ahead, s_m2, s_p2)
    q = jnp.where(ahead, s_m1, s_p1)
    r = s_0
    w = jnp.where(ahead, s_p1, s_m1)
    k = 13.0 / 3.0
    a1, b1 = p - q, p - 3.0 * q
    a2, b2 = q - r, q + r
    a3, b3 = r - w, 3.0 * r - w
    t1 = k * (a1 * a1) + (b1 * b1 + EPS4)
    t2 = k * (a2 * a2) + (b2 * b2 + EPS4)
    t3 = k * (a3 * a3) + (b3 * b3 + EPS4)
    m1, m2, m3 = t2 * t3, t1 * t3, t1 * t2
    w1 = m1 * m1
    w2 = 6.0 * (m2 * m2)
    w3 = 3.0 * (m3 * m3)
    top = w1 * (2.0 * p - 5.0 * q) - w2 * (q + 2.0 * r) + w3 * (w - 4.0 * r)
    bottom = w1 + w2 + w3
    return speed * c - (jnp.abs(speed) * (1.0 / 6.0)) * (top / bottom)


def step_term(field, row, u, v):
    window = field[pl.ds(pl.multiple_of(row - 8, 8), 24), :]
    taps = [pltpu.roll(window, (24 - k) % 24, 0)[8:16] for k in range(-3, 4)]
    here = taps[3]
    width = here.shape[1]
    d = [taps[k + 1] - taps[k] for k in range(6)]
    s = [d[k + 1] - d[k] for k in range(5)]
    along_y = one_sided(v, d[2], d[3], *s)
    upper = pltpu.roll(here, width - 1, 1) - here
    lower = here - pltpu.roll(here, 1, 1)
    mid = upper - lower
    along_x = one_sided(
        u,
        lower,
        upper,
        pltpu.roll(mid, 2, 1),
        pltpu.roll(mid, 1, 1),
        mid,
        pltpu.roll(mid, width - 1, 1),
        pltpu.roll(mid, width - 2, 1),
    )
    return here, -(along_x + along_y)


def kernel(
    nb,
    nx,
    level_hbm,
    flow_hbm,
    parts_hbm,
    escaped_hbm,
    home_ref,
    land_ref,
    dest_ref,
    count_ref,
    out_ref,
    moved_hbm,
    f0,
    flow,
    f1,
    f2,
    side,
    from_left,
    from_right,
    parts,
    escaped,
    packed,
    records,
    rec_same,
    rec_left,
    load_sem,
    halo_send,
    halo_recv,
    pay_send,
    pay_recv,
    rec_send,
    rec_recv,
    left_send,
    left_recv,
    own_sem,
):
    g = lax.axis_index("gy")
    s = lax.axis_index("gx")
    height, across = level_hbm.shape
    width = across + LANES
    total = parts_hbm.shape[0]
    up = lax.rem(g + nb - 1, nb)
    down = lax.rem(g + 1, nb)
    left = lax.rem(s + nx - 1, nx)
    right = lax.rem(s + 1, nx)

    barrier = pltpu.get_barrier_semaphore()
    offsets = sorted({0, 1 % nx, (nx - 1) % nx})
    for off in offsets:
        strip = lax.rem(s + off, nx)

        def greet(k, carry, strip=strip):
            pl.semaphore_signal(
                barrier, inc=1, device_id=(lax.rem(g + k, nb), strip), device_id_type=MESH
            )
            return carry

        lax.fori_loop(1 if off == 0 else 0, nb, greet, 0)

    loads = [
        pltpu.make_async_copy(
            level_hbm, f0.at[pl.ds(DEEP, height), pl.ds(0, across)], load_sem.at[0]
        ),
        pltpu.make_async_copy(
            flow_hbm, flow.at[:, pl.ds(THIN, height), pl.ds(0, across)], load_sem.at[1]
        ),
        pltpu.make_async_copy(parts_hbm, parts, load_sem.at[2]),
        pltpu.make_async_copy(escaped_hbm, escaped, load_sem.at[3]),
    ]
    for copy in loads:
        copy.start()

    home = home_ref[...].reshape(1, total)
    land = land_ref[...].reshape(1, total)
    dest = dest_ref[...].reshape(1, total)
    lane = lax.broadcasted_iota(jnp.int32, (total, total), 1)
    sub = lax.broadcasted_iota(jnp.int32, (total, total), 0)

    def upright(row):
        return jnp.sum(jnp.where(lane == sub, row, 0), axis=1, keepdims=True)

    dest_col = upright(dest)
    home_col = upright(home)
    land_col = upright(land)
    live = count_ref[0]
    earlier = (dest == dest_col) & (sub < lane) & (sub < live)
    rank = jnp.sum(earlier.astype(jnp.int32), axis=0, keepdims=True)
    is_live = lax.broadcasted_iota(jnp.int32, (1, total), 1) < live
    slot = jnp.where(is_live, dest * (CAP * FIELDS) + rank * FIELDS, -64)
    own_row = jnp.where(is_live, dest * (2 * CAP) + rank, -64)
    next_band = jnp.where(dest == nb - 1, 0, dest + 1)
    past_row = jnp.where(is_live, next_band * (2 * CAP) + CAP + rank, -64)

    loads[0].wait()
    loads[1].wait()

    spot = lax.broadcasted_iota(jnp.int32, (height, LANES), 1)
    low = [
        f0[pl.ds(DEEP, height), 0:LANES],
        pltpu.roll(flow[0, pl.ds(THIN, height), 0:LANES], 16, 1),
        pltpu.roll(flow[1, pl.ds(THIN, height), 0:LANES], 32, 1),
    ]
    tail = pl.ds(across - LANES, LANES)
    high = [
        f0[pl.ds(DEEP, height), tail],
        pltpu.roll(flow[0, pl.ds(THIN, height), tail], LANES - 16, 1),
        pltpu.roll(flow[1, pl.ds(THIN, height), tail], LANES - 32, 1),
    ]
    low_edge = jnp.where(spot < 16, low[0], jnp.where(spot < 32, low[1], low[2]))
    high_edge = jnp.where(spot >= 112, high[0], jnp.where(spot >= 96, high[1], high[2]))
    side[...] = jnp.where(spot < 64, low_edge, high_edge)

    pl.semaphore_wait(barrier, nb * len(offsets) - 1)

    halo = []

    def send(src, dst, band, strip):
        i = len(halo)
        copy = pltpu.make_async_remote_copy(
            src_ref=src,
            dst_ref=dst,
            send_sem=halo_send.at[i],
            recv_sem=halo_recv.at[i],
            device_id=(band, strip),
            device_id_type=MESH,
        )
        copy.start()
        halo.append(copy)

    wide = pl.ds(0, across)
    for box, strip in ((from_right, left), (from_left, right))[: 2 if nx > 2 else 1]:
        send(side, box.at[pl.ds(DEEP, height)], g, strip)
        send(side.at[pl.ds(0, DEEP)], box.at[pl.ds(DEEP + height, DEEP)], up, strip)
        send(side.at[pl.ds(height - DEEP, DEEP)], box.at[pl.ds(0, DEEP)], down, strip)
    send(
        flow_hbm.at[:, pl.ds(0, THIN)], flow.at[:, pl.ds(THIN + height, THIN), wide], up, s
    )
    send(
        flow_hbm.at[:, pl.ds(height - THIN, THIN)], flow.at[:, pl.ds(0, THIN), wide], down, s
    )
    send(level_hbm.at[pl.ds(0, DEEP)], f0.at[pl.ds(DEEP + height, DEEP), wide], up, s)
    send(level_hbm.at[pl.ds(height - DEEP, DEEP)], f0.at[pl.ds(0, DEEP), wide], down, s)

    loads[2].wait()
    loads[3].wait()
    radius = parts[:, 2, :]
    weight = escaped[...].astype(jnp.float32) * radius

    home_row = home_col // across
    home_at = home_col - home_row * across
    pick_lane = lax.broadcasted_iota(jnp.int32, (total, THIN + height), 1)
    pick_this = (pick_lane == home_row).astype(jnp.float32)
    pick_next = (pick_lane == home_row + 1).astype(jnp.float32)

    for copy in halo:
        copy.wait()

    spot = lax.broadcasted_iota(jnp.int32, (height + 2 * DEEP, LANES), 1)
    after = from_right[...]
    before = from_left[...] if nx > 2 else after
    end = pl.ds(across, LANES)
    f0[:, end] = jnp.where(spot < 64, after, before)
    inner = slice(DEEP - THIN, DEEP + height + THIN)
    spot, after, before = spot[inner], after[inner], before[inner]
    flow[0, :, end] = jnp.where(
        spot < 64, pltpu.roll(after, LANES - 16, 1), pltpu.roll(before, 16, 1)
    )
    flow[1, :, end] = jnp.where(
        spot < 64, pltpu.roll(after, LANES - 32, 1), pltpu.roll(before, 32, 1)
    )

    column = lax.broadcasted_iota(jnp.int32, (total, width), 1)
    this_column = column == home_at
    next_column = column == home_at + 1

    fraction_y = parts[:, 1, :] + 0.5
    fraction_x = parts[:, 0, :] + 0.5

    def mixture(component):
        cells = flow[component, pl.ds(THIN, height + THIN), :]
        this_row = jnp.dot(
            pick_this, cells, precision=EXACT, preferred_element_type=jnp.float32
        )
        next_row = jnp.dot(
            pick_next, cells, precision=EXACT, preferred_element_type=jnp.float32
        )

        def at(rows, mask):
            return jnp.sum(jnp.where(mask, rows, 0.0), axis=1, keepdims=True)

        return (
            (1.0 - fraction_y) * (1.0 - fraction_x) * at(this_row, this_column)
            + fraction_y * (1.0 - fraction_x) * at(next_row, this_column)
            + (1.0 - fraction_y) * fraction_x * at(this_row, next_column)
            + fraction_y * fraction_x * at(next_row, next_column)
        )

    new_x = parts[:, 0, :] + STEP * mixture(0)
    new_y = parts[:, 1, :] + STEP * mixture(1)

    slot_row = lax.broadcasted_iota(jnp.int32, (nb * CAP * FIELDS, total), 0)
    payload = None
    for k, rows in enumerate((new_x, new_y, radius, weight)):
        term = jnp.dot(
            (slot_row == slot + k).astype(jnp.float32),
            rows,
            precision=EXACT,
            preferred_element_type=jnp.float32,
        )
        payload = term if payload is None else payload + term
    packed[...] = payload

    gy = new_y + 0.5
    gx = new_x + 0.5

    def over(rows):
        return jnp.sum(rows, axis=1, keepdims=True)

    land_row = land_col // across
    columns = (
        land_row.astype(jnp.float32),
        (land_col - land_row * across).astype(jnp.float32),
        over(weight * (1.0 - gy) * (1.0 - gx)),
        over(weight * gy * (1.0 - gx)),
        over(weight * (1.0 - gy) * gx),
        over(weight * gy * gx),
    )
    spot = lax.broadcasted_iota(jnp.int32, (total, LANES), 1)
    table = jnp.zeros((total, LANES), jnp.float32)
    for k, one in enumerate(columns):
        table = jnp.where(spot == k, one, table)
    rec_row = lax.broadcasted_iota(jnp.int32, (nb * 2 * CAP, total), 0)
    records[...] = jnp.dot(
        ((rec_row == own_row) | (rec_row == past_row)).astype(jnp.float32),
        table,
        precision=EXACT,
        preferred_element_type=jnp.float32,
    )

    per = CAP * FIELDS
    two = 2 * CAP
    mine = pl.ds(pl.multiple_of(g * per, per), per)
    mine_rec = pl.ds(pl.multiple_of(g * two, two), two)

    def pay_copy(k):
        peer = lax.rem(g + k, nb)
        return pltpu.make_async_remote_copy(
            src_ref=packed.at[pl.ds(pl.multiple_of(peer * per, per), per)],
            dst_ref=moved_hbm.at[mine],
            send_sem=pay_send.at[k],
            recv_sem=pay_recv.at[k],
            device_id=(peer, s),
            device_id_type=MESH,
        )

    def rec_copy(k):
        peer = lax.rem(g + k, nb)
        return pltpu.make_async_remote_copy(
            src_ref=records.at[pl.ds(pl.multiple_of(peer * two, two), two)],
            dst_ref=rec_same.at[mine_rec],
            send_sem=rec_send.at[k],
            recv_sem=rec_recv.at[k],
            device_id=(peer, s),
            device_id_type=MESH,
        )

    def left_copy(k):
        peer = lax.rem(g + k, nb)
        return pltpu.make_async_remote_copy(
            src_ref=records.at[pl.ds(pl.multiple_of(peer * two, two), two)],
            dst_ref=rec_left.at[mine_rec],
            send_sem=left_send.at[k],
            recv_sem=left_recv.at[k],
            device_id=(peer, right),
            device_id_type=MESH,
        )

    def start_far(k, carry):
        rec_copy(k).start()
        left_copy(k).start()
        pay_copy(k).start()
        return carry

    left_copy(0).start()
    lax.fori_loop(1, nb, start_far, 0)
    own = [
        pltpu.make_async_copy(packed.at[mine], moved_hbm.at[mine], own_sem.at[0]),
        pltpu.make_async_copy(records.at[mine_rec], rec_same.at[mine_rec], own_sem.at[1]),
    ]
    for copy in own:
        copy.start()

    def first(i, carry):
        row = pl.multiple_of(i * 8, 8)
        here, term = step_term(
            f0, row + DEEP - THIN, flow[0, pl.ds(row, 8), :], flow[1, pl.ds(row, 8), :]
        )
        f1[pl.ds(row + DEEP - THIN, 8), :] = here + STEP * term
        return carry

    lax.fori_loop(0, (height + 2 * THIN) // 8, first, 0)

    def second(i, carry):
        row = pl.multiple_of(i * 8, 8)
        here, term = step_term(
            f1, row + DEEP - THIN, flow[0, pl.ds(row, 8), :], flow[1, pl.ds(row, 8), :]
        )
        at = pl.ds(row + DEEP - THIN, 8)
        f2[at, :] = 0.75 * f0[at, :] + 0.25 * (here + STEP * term)
        return carry

    lax.fori_loop(0, (height + 2 * THIN) // 8, second, 0)

    def third(i, carry):
        row = pl.multiple_of(i * 8, 8)
        at = pl.ds(row + THIN, 8)
        here, term = step_term(f2, row + DEEP, flow[0, at, :], flow[1, at, :])
        value = f0[pl.ds(row + DEEP, 8), :] / 3.0 + 2.0 / 3.0 * (here + STEP * term)
        out_ref[pl.ds(row, 8), :] = value[:, :across]
        return carry

    lax.fori_loop(0, height // 8, third, 0)

    for copy in own:
        copy.wait()
    left_copy(0).wait()

    def finish_far(k, carry):
        rec_copy(k).wait()
        left_copy(k).wait()
        return carry

    lax.fori_loop(1, nb, finish_far, 0)

    count = nb * two
    row_lane = lax.broadcasted_iota(jnp.int32, (count, LANES), 1)
    which = lax.broadcasted_iota(jnp.int32, (count, 1), 0)
    shift = jnp.where(lax.rem(which, two) >= CAP, float(height), 0.0)
    row_lane = row_lane.astype(jnp.float32)
    lane_out = lax.broadcasted_iota(jnp.int32, (count, across), 1).astype(jnp.float32)

    def laid(hot, rows):
        return lax.dot_general(
            hot.astype(jnp.float32),
            rows,
            (((0,), (0,)), ((), ())),
            precision=EXACT,
            preferred_element_type=jnp.float32,
        )[:height]

    box = rec_same[...]
    row_of = box[:, 0:1] - shift
    col_of = box[:, 1:2]
    at_col = lane_out == col_of
    at_next = lane_out == col_of + 1.0
    same_low = jnp.where(at_col, box[:, 2:3], jnp.where(at_next, box[:, 4:5], 0.0))
    same_high = jnp.where(at_col, box[:, 3:4], jnp.where(at_next, box[:, 5:6], 0.0))
    out_ref[...] += laid(row_lane == row_of, same_low) + laid(
        row_lane == row_of + 1.0, same_high
    )
    box = rec_left[...]
    row_of = box[:, 0:1] - shift
    spill = (box[:, 1:2] == float(across - 1)) & (row_lane == 0.0)
    left_low = jnp.where(spill, box[:, 4:5], 0.0)
    left_high = jnp.where(spill, box[:, 5:6], 0.0)
    out_ref[:, 0:LANES] += laid(row_lane == row_of, left_low) + laid(
        row_lane == row_of + 1.0, left_high
    )

    def finish_pay(k, carry):
        pay_copy(k).wait()
        return carry

    lax.fori_loop(1, nb, finish_pay, 0)


def shards(nb, nx, level_set, velocity, particles, escaped, home, land, dest, count):
    height, across = level_set.shape
    total, _, per_block = particles.shape
    width = across + LANES
    rows = nb * CAP * FIELDS
    recs = nb * 2 * CAP
    halos = 10 if nx > 2 else 7
    anywhere = pl.BlockSpec(memory_space=pl.ANY)
    vmem = pl.BlockSpec(memory_space=pltpu.VMEM)
    smem = pl.BlockSpec(memory_space=pltpu.SMEM)
    f32 = jnp.float32
    dma = pltpu.SemaphoreType.DMA
    level, moved = pl.pallas_call(
        functools.partial(kernel, nb, nx),
        out_shape=(
            jax.ShapeDtypeStruct((height, across), f32),
            jax.ShapeDtypeStruct((rows, per_block), f32),
        ),
        in_specs=[anywhere] * 4 + [vmem] * 3 + [smem],
        out_specs=(vmem, anywhere),
        scratch_shapes=[
            pltpu.VMEM((height + 2 * DEEP, width), f32),
            pltpu.VMEM((2, height + 2 * THIN, width), f32),
            pltpu.VMEM((height + 2 * DEEP, width), f32),
            pltpu.VMEM((height + 2 * DEEP, width), f32),
            pltpu.VMEM((height, LANES), f32),
            pltpu.VMEM((height + 2 * DEEP, LANES), f32),
            pltpu.VMEM((height + 2 * DEEP, LANES), f32),
            pltpu.VMEM(particles.shape, f32),
            pltpu.VMEM(escaped.shape, jnp.int32),
            pltpu.VMEM((rows, per_block), f32),
            pltpu.VMEM((recs, LANES), f32),
            pltpu.VMEM((recs, LANES), f32),
            pltpu.VMEM((recs, LANES), f32),
            dma((4,)),
            dma((halos,)),
            dma((halos,)),
            dma((nb,)),
            dma((nb,)),
            dma((nb,)),
            dma((nb,)),
            dma((nb,)),
            dma((nb,)),
            dma((2,)),
        ],
        compiler_params=pltpu.CompilerParams(collective_id=0, has_side_effects=True),
    )(level_set, velocity, particles, escaped, home, land, dest, count)
    return level, moved.reshape(nb * CAP, FIELDS, per_block)


def solution(mesh):
    in_specs = (
        P("gy", "gx"),
        P(None, "gy", "gx"),
        P(("gy", "gx"), None, None),
        P(("gy", "gx"), None),
        P(("gy", "gx")),
        P(("gy", "gx")),
        P(("gy", "gx")),
        P(("gy", "gx")),
    )
    out_specs = (P("gy", "gx"), P(("gy", "gx"), None, None))
    body = functools.partial(shards, mesh.shape["gy"], mesh.shape["gx"])
    return jax.shard_map(body, mesh=mesh, in_specs=in_specs, out_specs=out_specs, check_vma=False)
```

time: 96.1 us -> 26.7 us (0.28)
  local copies, waits for them, and re-layouts: 38 us -> 3.88 us
  Pallas kernels: 0 us -> 21.4 us
  other arithmetic: 19.5 us -> 0 us
  waiting for transfers between devices: 19.4 us -> 0 us
  starting transfers between devices: 16.6 us -> 0 us
    gather x8 -> x0, local copies, waits for them, and re-layouts: 26.1 us -> none  [the longest x2 6.53 us: shards(): flattened[:, home_flat + across + 1]]
    pallas_call x0 -> x1, Pallas kernels: none -> 21.4 us  [shards(): pl.pallas_call(functools.partial(kernel, nb, nx), out_shape=(jax.ShapeDty...]
    all_to_all x2 -> x0, waiting for transfers between devices: 11.7 us -> none  [the longest x1 7.49 us: shards(): lax.all_to_all(packed, 'gy', split_axis=0, concat_axis=0, tiled=True)]
    ppermute x6 -> x0, starting transfers between devices: 9.47 us -> none  [the longest x2 6.82 us: with_halo(): lax.ppermute(head, axis, [((i + 1) % count, i) for i in range(count)])]
    reshape x6 -> x0, local copies, waits for them, and re-layouts: 9.28 us -> none  [the longest x2 8.87 us: shards(): flattened = corner_flow.reshape(2, -1)]
    ppermute x6 -> x0, waiting for transfers between devices: 7.75 us -> none  [the longest x2 4.43 us: with_halo(): lax.ppermute(head, axis, [((i + 1) % count, i) for i in range(count)])]
    all_to_all x2 -> x0, starting transfers between devices: 7.13 us -> none  [the longest x1 3.62 us: shards(): lax.all_to_all(cell_out, 'gy', split_axis=0, concat_axis=0, tiled=True)]
    add x5 -> x0, other arithmetic: 6.46 us -> none  [the longest x1 2.2 us: shards(): surface[3:-3, 3:-3]]
  transfers between devices with their start and end apart: 8 -> 0, of which waited for: 4 -> 0; matrix products, arithmetic and copies ran while one was open for 50% -> 0% of each run, Pallas kernels for 0% -> 0%
where the time goes in v1:
time: 26.7 us; the launch traced here: 26.5 us
  Pallas kernels  21.4 us (80%)
  local copies, waits for them, and re-layouts  3.88 us (15%)
  between operations  1.29 us (5%)
    pallas_call x1, Pallas kernels, shards(): pl.pallas_call(functools.partial(kernel, nb, nx), out_shape=(jax.ShapeDty...  21.4 us
    unnamed x5, local copies, waits for them, and re-layouts  3.88 us

profile of v1, /device:TPU:0, one launch (start us, length us, event | category | flops | bytes accessed | tf_op | source)
XLA Modules:
  0.0 26.5 jit_solution(5781884645743930845)
XLA Ops:
  1.3 1.6 %copy.10.parts_hbm = f32[64,3,128]{2,1,0:T(4,128)} copy(f32[64,3,128]{2,0,1:T(8,128)} %param.10) | data formatting | bytes 196608 | tf_op args[2]
  2.9 21.4 %shard_map.95 = (f32[64,512]{1,0:T(8,128)}, f32[256,128]{1,0:T(8,128)}) custom-call(f32[64,512]{1,0:T(8,128)} %level_hbm.1, f32[2,64,512]{2,1,0:T(8,128)} %flow_hbm.1, f32[64,3,128]{2,1,0:T(4,128)} %copy.10.parts_hbm, s32[64,128]{1,0:T(8,128)} %escaped_hbm.1, s32[64]{0:T(128)} %home_ref.1, s32[64]{0:T(128)} %land_ref.1, s32[64]{0:T(128)} %dest_ref.1, ...), custom_call_target="tpu_custom_call" | custom-call | tf_op jit(solution)/shard_map/pallas_call | solution.py:457
  24.3 0.0 copy-start
  24.3 1.6 %copy.14 = f32[64,512]{1,0:T(8,128)} copy(f32[64,512]{1,0:T(8,128)} %get-tuple-element.8) | data formatting | bytes 262144
  25.9 0.0 copy-done
  25.9 0.7 %copy.15 = f32[64,4,128]{2,1,0:T(4,128)} copy(f32[64,4,128]{2,1,0:T(4,128)S(1)} %bitcast.1) | data formatting | bytes 262144
Async XLA Ops:
  24.3 1.6 %copy-start = (f32[256,128]{1,0:T(8,128)S(1)}, f32[256,128]{1,0:T(8,128)}, u32[]{:S(2)}) copy-start(f32[256,128]{1,0:T(8,128)} %get-tuple-element.5) | copy-start | bytes 393220

commit v2 on v1

--- a/solution.py
+++ b/solution.py
@@ -106,7 +106,7 @@
     s = lax.axis_index("gx")
     height, across = level_hbm.shape
     width = across + LANES
-    total = parts_hbm.shape[0]
+    total = parts_hbm.shape[1]
     up = lax.rem(g + nb - 1, nb)
     down = lax.rem(g + 1, nb)
     left = lax.rem(s + nx - 1, nx)
@@ -211,7 +211,7 @@
 
     loads[2].wait()
     loads[3].wait()
-    radius = parts[:, 2, :]
+    radius = parts[2]
     weight = escaped[...].astype(jnp.float32) * radius
 
     home_row = home_col // across
@@ -241,8 +241,8 @@
     this_column = column == home_at
     next_column = column == home_at + 1
 
-    fraction_y = parts[:, 1, :] + 0.5
-    fraction_x = parts[:, 0, :] + 0.5
+    fraction_y = parts[1] + 0.5
+    fraction_x = parts[0] + 0.5
 
     def mixture(component):
         cells = flow[component, pl.ds(THIN, height + THIN), :]
@@ -263,8 +263,8 @@
             + fraction_y * fraction_x * at(next_row, next_column)
         )
 
-    new_x = parts[:, 0, :] + STEP * mixture(0)
-    new_y = parts[:, 1, :] + STEP * mixture(1)
+    new_x = parts[0] + STEP * mixture(0)
+    new_y = parts[1] + STEP * mixture(1)
 
     slot_row = lax.broadcasted_iota(jnp.int32, (nb * CAP * FIELDS, total), 0)
     payload = None
@@ -444,7 +444,7 @@
 
 def shards(nb, nx, level_set, velocity, particles, escaped, home, land, dest, count):
     height, across = level_set.shape
-    total, _, per_block = particles.shape
+    total, kinds, per_block = particles.shape
     width = across + LANES
     rows = nb * CAP * FIELDS
     recs = nb * 2 * CAP
@@ -457,11 +457,11 @@
     level, moved = pl.pallas_call(
         functools.partial(kernel, nb, nx),
         out_shape=(
-            jax.ShapeDtypeStruct((height, across), f32),
-            jax.ShapeDtypeStruct((rows, per_block), f32),
+            pltpu.VMEM((height, across), f32),
+            pltpu.VMEM((rows, per_block), f32),
         ),
         in_specs=[anywhere] * 4 + [vmem] * 3 + [smem],
-        out_specs=(vmem, anywhere),
+        out_specs=(vmem, vmem),
         scratch_shapes=[
             pltpu.VMEM((height + 2 * DEEP, width), f32),
             pltpu.VMEM((2, height + 2 * THIN, width), f32),
@@ -470,7 +470,7 @@
             pltpu.VMEM((height, LANES), f32),
             pltpu.VMEM((height + 2 * DEEP, LANES), f32),
             pltpu.VMEM((height + 2 * DEEP, LANES), f32),
-            pltpu.VMEM(particles.shape, f32),
+            pltpu.VMEM((kinds, total, per_block), f32),
             pltpu.VMEM(escaped.shape, jnp.int32),
             pltpu.VMEM((rows, per_block), f32),
             pltpu.VMEM((recs, LANES), f32),
@@ -488,7 +488,16 @@
             dma((2,)),
         ],
         compiler_params=pltpu.CompilerParams(collective_id=0, has_side_effects=True),
-    )(level_set, velocity, particles, escaped, home, land, dest, count)
+    )(
+        level_set,
+        velocity,
+        jnp.transpose(particles, (1, 0, 2)),
+        escaped,
+        home,
+        land,
+        dest,
+        count,
+    )
     return level, moved.reshape(nb * CAP, FIELDS, per_block)
 
 

time: 26.7 us -> 23.5 us (0.88)
  local copies, waits for them, and re-layouts: 3.88 us -> 1.31 us
  Pallas kernels: 21.4 us -> 20.7 us
    unnamed x5 -> x2, local copies, waits for them, and re-layouts: 3.88 us -> 1.31 us
    pallas_call x1, Pallas kernels: 21.4 us -> 20.7 us  [shards(): pl.pallas_call(functools.partial(kernel, nb, nx), out_shape=(pltpu.VMEM((...]
where the time goes in v2:
time: 23.5 us; the launch traced here: 23.3 us
  Pallas kernels  20.7 us (88%)
  local copies, waits for them, and re-layouts  1.31 us (6%)
  between operations  1.29 us (5%)
    pallas_call x1, Pallas kernels, shards(): pl.pallas_call(functools.partial(kernel, nb, nx), out_shape=(pltpu.VMEM((...  20.7 us
    unnamed x2, local copies, waits for them, and re-layouts  1.31 us

profile of v2, /device:TPU:0, one launch (start us, length us, event | category | flops | bytes accessed | tf_op | source)
XLA Modules:
  0.0 23.3 jit_solution(15986765735575917088)
XLA Ops:
  1.3 20.7 %shard_map.95 = (f32[64,512]{1,0:T(8,128)S(1)}, f32[256,128]{1,0:T(8,128)S(1)}) custom-call(f32[64,512]{1,0:T(8,128)} %level_hbm.1, f32[2,64,512]{2,1,0:T(8,128)} %flow_hbm.1, f32[3,64,128]{2,1,0:T(8,128)} %bitcast.3, s32[64,128]{1,0:T(8,128)} %escaped_hbm.1, s32[64]{0:T(128)} %home_ref.1, s32[64]{0:T(128)} %land_ref.1, s32[64]{0:T(128)} %dest_ref.1, ...), custom_call_target="tpu_custom_call" | custom-call | tf_op jit(solution)/shard_map/pallas_call | solution.py:457
  22.0 0.7 %copy.12 = f32[64,512]{1,0:T(8,128)} copy(f32[64,512]{1,0:T(8,128)S(1)} %get-tuple-element.6) | data formatting | bytes 262144
  22.6 0.7 %copy.13 = f32[64,4,128]{2,1,0:T(4,128)} copy(f32[64,4,128]{2,1,0:T(4,128)S(1)} %bitcast.2) | data formatting | bytes 262144

commit v3 on v2

--- a/solution.py
+++ b/solution.py
@@ -15,7 +15,6 @@
 DEEP = 16
 THIN = 8
 MESH = pl.DeviceIdType.MESH
-EXACT = lax.Precision.HIGHEST
 
 
 def one_sided(speed, lower, upper, s_m2, s_m1, s_0, s_p1, s_p2):
@@ -65,6 +64,21 @@
     return here, -(along_x + along_y)
 
 
+def pieces(x):
+    top = x.astype(jnp.bfloat16)
+    rest = x - top.astype(jnp.float32)
+    middle = rest.astype(jnp.bfloat16)
+    return top, middle, (rest - middle.astype(jnp.float32)).astype(jnp.bfloat16)
+
+
+def chosen(hot, x):
+    hot = hot.astype(jnp.bfloat16)
+    top, middle, last = (
+        jnp.dot(hot, part, preferred_element_type=jnp.float32) for part in pieces(x)
+    )
+    return top + (middle + last)
+
+
 def kernel(
     nb,
     nx,
@@ -72,10 +86,10 @@
     flow_hbm,
     parts_hbm,
     escaped_hbm,
-    home_ref,
-    land_ref,
-    dest_ref,
-    count_ref,
+    home_hbm,
+    land_hbm,
+    dest_hbm,
+    count_hbm,
     out_ref,
     moved_hbm,
     f0,
@@ -87,6 +101,10 @@
     from_right,
     parts,
     escaped,
+    home_ref,
+    land_ref,
+    dest_ref,
+    count_ref,
     packed,
     records,
     rec_same,
@@ -135,8 +153,21 @@
         pltpu.make_async_copy(parts_hbm, parts, load_sem.at[2]),
         pltpu.make_async_copy(escaped_hbm, escaped, load_sem.at[3]),
     ]
-    for copy in loads:
+    small = [
+        pltpu.make_async_copy(src, dst, load_sem.at[4 + k])
+        for k, (src, dst) in enumerate(
+            (
+                (home_hbm, home_ref),
+                (land_hbm, land_ref),
+                (dest_hbm, dest_ref),
+                (count_hbm, count_ref),
+            )
+        )
+    ]
+    for copy in small + loads:
         copy.start()
+    for copy in small:
+        copy.wait()
 
     home = home_ref[...].reshape(1, total)
     land = land_ref[...].reshape(1, total)
@@ -154,10 +185,10 @@
     earlier = (dest == dest_col) & (sub < lane) & (sub < live)
     rank = jnp.sum(earlier.astype(jnp.int32), axis=0, keepdims=True)
     is_live = lax.broadcasted_iota(jnp.int32, (1, total), 1) < live
-    slot = jnp.where(is_live, dest * (CAP * FIELDS) + rank * FIELDS, -64)
-    own_row = jnp.where(is_live, dest * (2 * CAP) + rank, -64)
-    next_band = jnp.where(dest == nb - 1, 0, dest + 1)
-    past_row = jnp.where(is_live, next_band * (2 * CAP) + CAP + rank, -64)
+    slot = jnp.where(is_live, dest * CAP + rank, -1)
+    rank_col = upright(rank)
+    own_band = jnp.where(is_live, dest, -1)
+    past_band = jnp.where(is_live, jnp.where(dest == nb - 1, 0, dest + 1), -1)
 
     loads[0].wait()
     loads[1].wait()
@@ -217,10 +248,21 @@
     home_row = home_col // across
     home_at = home_col - home_row * across
     pick_lane = lax.broadcasted_iota(jnp.int32, (total, THIN + height), 1)
-    pick_this = (pick_lane == home_row).astype(jnp.float32)
-    pick_next = (pick_lane == home_row + 1).astype(jnp.float32)
-
-    for copy in halo:
+    pick = jnp.concatenate(
+        [
+            (pick_lane == home_row).astype(jnp.float32),
+            (pick_lane == home_row + 1).astype(jnp.float32),
+        ],
+        axis=0,
+    )
+    slot_row = lax.broadcasted_iota(jnp.int32, (nb * CAP, total), 0)
+    slot_hot = (slot_row == slot).astype(jnp.float32)
+    band_row = lax.broadcasted_iota(jnp.int32, (nb, total), 0)
+    own_hot = (band_row == own_band).astype(jnp.float32)
+    past_hot = (band_row == past_band).astype(jnp.float32)
+    land_row = land_col // across
+
+    for copy in halo[:-2]:
         copy.wait()
 
     spot = lax.broadcasted_iota(jnp.int32, (height + 2 * DEEP, LANES), 1)
@@ -246,12 +288,8 @@
 
     def mixture(component):
         cells = flow[component, pl.ds(THIN, height + THIN), :]
-        this_row = jnp.dot(
-            pick_this, cells, precision=EXACT, preferred_element_type=jnp.float32
-        )
-        next_row = jnp.dot(
-            pick_next, cells, precision=EXACT, preferred_element_type=jnp.float32
-        )
+        both = chosen(pick, cells)
+        this_row, next_row = both[:total], both[total:]
 
         def at(rows, mask):
             return jnp.sum(jnp.where(mask, rows, 0.0), axis=1, keepdims=True)
@@ -266,17 +304,9 @@
     new_x = parts[0] + STEP * mixture(0)
     new_y = parts[1] + STEP * mixture(1)
 
-    slot_row = lax.broadcasted_iota(jnp.int32, (nb * CAP * FIELDS, total), 0)
-    payload = None
-    for k, rows in enumerate((new_x, new_y, radius, weight)):
-        term = jnp.dot(
-            (slot_row == slot + k).astype(jnp.float32),
-            rows,
-            precision=EXACT,
-            preferred_element_type=jnp.float32,
-        )
-        payload = term if payload is None else payload + term
-    packed[...] = payload
+    payload = chosen(slot_hot, jnp.concatenate([new_x, new_y, radius, weight], axis=1))
+    for k in range(FIELDS):
+        packed[pl.ds(k, nb * CAP, stride=FIELDS), :] = payload[:, k * LANES : (k + 1) * LANES]
 
     gy = new_y + 0.5
     gx = new_x + 0.5
@@ -284,7 +314,6 @@
     def over(rows):
         return jnp.sum(rows, axis=1, keepdims=True)
 
-    land_row = land_col // across
     columns = (
         land_row.astype(jnp.float32),
         (land_col - land_row * across).astype(jnp.float32),
@@ -296,19 +325,16 @@
     spot = lax.broadcasted_iota(jnp.int32, (total, LANES), 1)
     table = jnp.zeros((total, LANES), jnp.float32)
     for k, one in enumerate(columns):
-        table = jnp.where(spot == k, one, table)
-    rec_row = lax.broadcasted_iota(jnp.int32, (nb * 2 * CAP, total), 0)
-    records[...] = jnp.dot(
-        ((rec_row == own_row) | (rec_row == past_row)).astype(jnp.float32),
-        table,
-        precision=EXACT,
-        preferred_element_type=jnp.float32,
-    )
+        table = jnp.where(spot // (2 * CAP) == k, one, table)
+    place = spot % (2 * CAP)
+    sheet = chosen(own_hot, jnp.where(place == rank_col, table, 0.0)) + chosen(
+        past_hot, jnp.where(place == rank_col + CAP, table, 0.0)
+    )
+    for band in range(nb):
+        records[band] = sheet[band : band + 1]
 
     per = CAP * FIELDS
-    two = 2 * CAP
     mine = pl.ds(pl.multiple_of(g * per, per), per)
-    mine_rec = pl.ds(pl.multiple_of(g * two, two), two)
 
     def pay_copy(k):
         peer = lax.rem(g + k, nb)
@@ -324,8 +350,8 @@
     def rec_copy(k):
         peer = lax.rem(g + k, nb)
         return pltpu.make_async_remote_copy(
-            src_ref=records.at[pl.ds(pl.multiple_of(peer * two, two), two)],
-            dst_ref=rec_same.at[mine_rec],
+            src_ref=records.at[peer],
+            dst_ref=rec_same.at[g],
             send_sem=rec_send.at[k],
             recv_sem=rec_recv.at[k],
             device_id=(peer, s),
@@ -335,8 +361,8 @@
     def left_copy(k):
         peer = lax.rem(g + k, nb)
         return pltpu.make_async_remote_copy(
-            src_ref=records.at[pl.ds(pl.multiple_of(peer * two, two), two)],
-            dst_ref=rec_left.at[mine_rec],
+            src_ref=records.at[peer],
+            dst_ref=rec_left.at[g],
             send_sem=left_send.at[k],
             recv_sem=left_recv.at[k],
             device_id=(peer, right),
@@ -353,10 +379,13 @@
     lax.fori_loop(1, nb, start_far, 0)
     own = [
         pltpu.make_async_copy(packed.at[mine], moved_hbm.at[mine], own_sem.at[0]),
-        pltpu.make_async_copy(records.at[mine_rec], rec_same.at[mine_rec], own_sem.at[1]),
+        pltpu.make_async_copy(records.at[g], rec_same.at[g], own_sem.at[1]),
     ]
     for copy in own:
         copy.start()
+
+    for copy in halo[-2:]:
+        copy.wait()
 
     def first(i, carry):
         row = pl.multiple_of(i * 8, 8)
@@ -400,40 +429,40 @@
 
     lax.fori_loop(1, nb, finish_far, 0)
 
-    count = nb * two
-    row_lane = lax.broadcasted_iota(jnp.int32, (count, LANES), 1)
-    which = lax.broadcasted_iota(jnp.int32, (count, 1), 0)
-    shift = jnp.where(lax.rem(which, two) >= CAP, float(height), 0.0)
-    row_lane = row_lane.astype(jnp.float32)
-    lane_out = lax.broadcasted_iota(jnp.int32, (count, across), 1).astype(jnp.float32)
-
-    def laid(hot, rows):
-        return lax.dot_general(
-            hot.astype(jnp.float32),
-            rows,
-            (((0,), (0,)), ((), ())),
-            precision=EXACT,
-            preferred_element_type=jnp.float32,
-        )[:height]
-
-    box = rec_same[...]
-    row_of = box[:, 0:1] - shift
-    col_of = box[:, 1:2]
-    at_col = lane_out == col_of
-    at_next = lane_out == col_of + 1.0
-    same_low = jnp.where(at_col, box[:, 2:3], jnp.where(at_next, box[:, 4:5], 0.0))
-    same_high = jnp.where(at_col, box[:, 3:4], jnp.where(at_next, box[:, 5:6], 0.0))
-    out_ref[...] += laid(row_lane == row_of, same_low) + laid(
-        row_lane == row_of + 1.0, same_high
-    )
-    box = rec_left[...]
-    row_of = box[:, 0:1] - shift
-    spill = (box[:, 1:2] == float(across - 1)) & (row_lane == 0.0)
-    left_low = jnp.where(spill, box[:, 4:5], 0.0)
-    left_high = jnp.where(spill, box[:, 5:6], 0.0)
-    out_ref[:, 0:LANES] += laid(row_lane == row_of, left_low) + laid(
-        row_lane == row_of + 1.0, left_high
-    )
+    row_lane = lax.broadcasted_iota(jnp.int32, (nb, LANES), 1).astype(jnp.float32)
+    lane_out = lax.broadcasted_iota(jnp.int32, (nb, across), 1).astype(jnp.float32)
+    spread = 2 * CAP
+
+    def slots_of(box):
+        for j in range(spread):
+            fields = [box[:, k * spread + j : k * spread + j + 1] for k in range(6)]
+            if j >= CAP:
+                fields[0] = fields[0] - float(height)
+            yield fields
+
+    def laid(hots, rows):
+        hot = jnp.transpose(jnp.concatenate(hots, axis=0))[:height]
+        return chosen(hot, jnp.concatenate(rows, axis=0))
+
+    hots, rows = [], []
+    for row, col, low_low, high_low, low_high, high_high in slots_of(
+        jnp.concatenate([rec_same[k] for k in range(nb)], axis=0)
+    ):
+        here, beside = lane_out == col, lane_out == col + 1.0
+        hots += [(row_lane == row).astype(jnp.float32), (row_lane == row + 1.0).astype(jnp.float32)]
+        rows += [
+            jnp.where(here, low_low, jnp.where(beside, low_high, 0.0)),
+            jnp.where(here, high_low, jnp.where(beside, high_high, 0.0)),
+        ]
+    out_ref[...] += laid(hots, rows)
+    hots, rows = [], []
+    for row, col, low_low, high_low, low_high, high_high in slots_of(
+        jnp.concatenate([rec_left[k] for k in range(nb)], axis=0)
+    ):
+        spill = (col == float(across - 1)) & (row_lane == 0.0)
+        hots += [(row_lane == row).astype(jnp.float32), (row_lane == row + 1.0).astype(jnp.float32)]
+        rows += [jnp.where(spill, low_high, 0.0), jnp.where(spill, high_high, 0.0)]
+    out_ref[:, 0:LANES] += laid(hots, rows)
 
     def finish_pay(k, carry):
         pay_copy(k).wait()
@@ -447,11 +476,8 @@
     total, kinds, per_block = particles.shape
     width = across + LANES
     rows = nb * CAP * FIELDS
-    recs = nb * 2 * CAP
     halos = 10 if nx > 2 else 7
-    anywhere = pl.BlockSpec(memory_space=pl.ANY)
     vmem = pl.BlockSpec(memory_space=pltpu.VMEM)
-    smem = pl.BlockSpec(memory_space=pltpu.SMEM)
     f32 = jnp.float32
     dma = pltpu.SemaphoreType.DMA
     level, moved = pl.pallas_call(
@@ -460,7 +486,7 @@
             pltpu.VMEM((height, across), f32),
             pltpu.VMEM((rows, per_block), f32),
         ),
-        in_specs=[anywhere] * 4 + [vmem] * 3 + [smem],
+        in_specs=[pl.BlockSpec(memory_space=pltpu.HBM)] * 8,
         out_specs=(vmem, vmem),
         scratch_shapes=[
             pltpu.VMEM((height + 2 * DEEP, width), f32),
@@ -472,11 +498,15 @@
             pltpu.VMEM((height + 2 * DEEP, LANES), f32),
             pltpu.VMEM((kinds, total, per_block), f32),
             pltpu.VMEM(escaped.shape, jnp.int32),
+            pltpu.VMEM(home.shape, jnp.int32),
+            pltpu.VMEM(land.shape, jnp.int32),
+            pltpu.VMEM(dest.shape, jnp.int32),
+            pltpu.SMEM(count.shape, jnp.int32),
             pltpu.VMEM((rows, per_block), f32),
-            pltpu.VMEM((recs, LANES), f32),
-            pltpu.VMEM((recs, LANES), f32),
-            pltpu.VMEM((recs, LANES), f32),
-            dma((4,)),
+            pltpu.VMEM((nb, 1, LANES), f32),
+            pltpu.VMEM((nb, 1, LANES), f32),
+            pltpu.VMEM((nb, 1, LANES), f32),
+            dma((8,)),
             dma((halos,)),
             dma((halos,)),
             dma((nb,)),

time: 23.5 us -> 21.7 us (0.923)
  Pallas kernels: 20.7 us -> 18.9 us
    pallas_call x1, Pallas kernels: 20.7 us -> 18.9 us  [shards(): pl.pallas_call(functools.partial(kernel, nb, nx), out_shape=(pltpu.VMEM((...]
where the time goes in v3:
time: 21.7 us; the launch traced here: 21.5 us
  Pallas kernels  18.9 us (87%)
  local copies, waits for them, and re-layouts  1.31 us (6%)
  between operations  1.29 us (6%)
    pallas_call x1, Pallas kernels, shards(): pl.pallas_call(functools.partial(kernel, nb, nx), out_shape=(pltpu.VMEM((...  18.9 us
    unnamed x2, local copies, waits for them, and re-layouts  1.31 us

profile of v3, /device:TPU:0, one launch (start us, length us, event | category | flops | bytes accessed | tf_op | source)
XLA Modules:
  0.0 21.5 jit_solution(2060311227811171659)
XLA Ops:
  1.3 18.9 %shard_map.95 = (f32[64,512]{1,0:T(8,128)S(1)}, f32[256,128]{1,0:T(8,128)S(1)}) custom-call(f32[64,512]{1,0:T(8,128)} %level_hbm.1, f32[2,64,512]{2,1,0:T(8,128)} %flow_hbm.1, f32[3,64,128]{2,1,0:T(8,128)} %bitcast.3, s32[64,128]{1,0:T(8,128)} %escaped_hbm.1, s32[64]{0:T(128)} %home_hbm.1, s32[64]{0:T(128)} %land_hbm.1, s32[64]{0:T(128)} %dest_hbm.1, ...), custom_call_target="tpu_custom_call" | custom-call | tf_op jit(solution)/shard_map/pallas_call | solution.py:483
  20.2 0.7 %copy.12 = f32[64,512]{1,0:T(8,128)} copy(f32[64,512]{1,0:T(8,128)S(1)} %get-tuple-element.6) | data formatting | bytes 262144
  20.8 0.7 %copy.13 = f32[64,4,128]{2,1,0:T(4,128)} copy(f32[64,4,128]{2,1,0:T(4,128)S(1)} %bitcast.2) | data formatting | bytes 262144

commit v4 on v3

--- a/solution.py
+++ b/solution.py
@@ -40,18 +40,20 @@
     return speed * c - (jnp.abs(speed) * (1.0 / 6.0)) * (top / bottom)
 
 
-def step_term(field, row, u, v):
-    window = field[pl.ds(pl.multiple_of(row - 8, 8), 24), :]
+def row_term(field, row, lanes, v):
+    window = field[pl.ds(pl.multiple_of(row - 8, 8), 24), lanes]
     taps = [pltpu.roll(window, (24 - k) % 24, 0)[8:16] for k in range(-3, 4)]
-    here = taps[3]
-    width = here.shape[1]
     d = [taps[k + 1] - taps[k] for k in range(6)]
     s = [d[k + 1] - d[k] for k in range(5)]
-    along_y = one_sided(v, d[2], d[3], *s)
+    return one_sided(v, d[2], d[3], *s)
+
+
+def column_term(here, u):
+    width = here.shape[1]
     upper = pltpu.roll(here, width - 1, 1) - here
     lower = here - pltpu.roll(here, 1, 1)
     mid = upper - lower
-    along_x = one_sided(
+    return one_sided(
         u,
         lower,
         upper,
@@ -61,7 +63,11 @@
         pltpu.roll(mid, width - 1, 1),
         pltpu.roll(mid, width - 2, 1),
     )
-    return here, -(along_x + along_y)
+
+
+def step_term(field, row, u, v):
+    here = field[pl.ds(pl.multiple_of(row, 8), 8), :]
+    return here, -(column_term(here, u) + row_term(field, row, slice(None), v))
 
 
 def pieces(x):
@@ -190,6 +196,33 @@
     own_band = jnp.where(is_live, dest, -1)
     past_band = jnp.where(is_live, jnp.where(dest == nb - 1, 0, dest + 1), -1)
 
+    pl.semaphore_wait(barrier, nb * len(offsets) - 1)
+
+    halo = []
+
+    def send(src, dst, band, strip):
+        i = len(halo)
+        copy = pltpu.make_async_remote_copy(
+            src_ref=src,
+            dst_ref=dst,
+            send_sem=halo_send.at[i],
+            recv_sem=halo_recv.at[i],
+            device_id=(band, strip),
+            device_id_type=MESH,
+        )
+        copy.start()
+        halo.append(copy)
+
+    wide = pl.ds(0, across)
+    send(
+        flow_hbm.at[:, pl.ds(0, THIN)], flow.at[:, pl.ds(THIN + height, THIN), wide], up, s
+    )
+    send(
+        flow_hbm.at[:, pl.ds(height - THIN, THIN)], flow.at[:, pl.ds(0, THIN), wide], down, s
+    )
+    send(level_hbm.at[pl.ds(0, DEEP)], f0.at[pl.ds(DEEP + height, DEEP), wide], up, s)
+    send(level_hbm.at[pl.ds(height - DEEP, DEEP)], f0.at[pl.ds(0, DEEP), wide], down, s)
+
     loads[0].wait()
     loads[1].wait()
 
@@ -209,37 +242,10 @@
     high_edge = jnp.where(spot >= 112, high[0], jnp.where(spot >= 96, high[1], high[2]))
     side[...] = jnp.where(spot < 64, low_edge, high_edge)
 
-    pl.semaphore_wait(barrier, nb * len(offsets) - 1)
-
-    halo = []
-
-    def send(src, dst, band, strip):
-        i = len(halo)
-        copy = pltpu.make_async_remote_copy(
-            src_ref=src,
-            dst_ref=dst,
-            send_sem=halo_send.at[i],
-            recv_sem=halo_recv.at[i],
-            device_id=(band, strip),
-            device_id_type=MESH,
-        )
-        copy.start()
-        halo.append(copy)
-
-    wide = pl.ds(0, across)
     for box, strip in ((from_right, left), (from_left, right))[: 2 if nx > 2 else 1]:
         send(side, box.at[pl.ds(DEEP, height)], g, strip)
         send(side.at[pl.ds(0, DEEP)], box.at[pl.ds(DEEP + height, DEEP)], up, strip)
         send(side.at[pl.ds(height - DEEP, DEEP)], box.at[pl.ds(0, DEEP)], down, strip)
-    send(
-        flow_hbm.at[:, pl.ds(0, THIN)], flow.at[:, pl.ds(THIN + height, THIN), wide], up, s
-    )
-    send(
-        flow_hbm.at[:, pl.ds(height - THIN, THIN)], flow.at[:, pl.ds(0, THIN), wide], down, s
-    )
-    send(level_hbm.at[pl.ds(0, DEEP)], f0.at[pl.ds(DEEP + height, DEEP), wide], up, s)
-    send(level_hbm.at[pl.ds(height - DEEP, DEEP)], f0.at[pl.ds(0, DEEP), wide], down, s)
-
     loads[2].wait()
     loads[3].wait()
     radius = parts[2]
@@ -262,7 +268,37 @@
     past_hot = (band_row == past_band).astype(jnp.float32)
     land_row = land_col // across
 
-    for copy in halo[:-2]:
+    column = lax.broadcasted_iota(jnp.int32, (total, across), 1)
+    this_column = column == home_at
+    next_column = column == home_at + 1
+    at_last = home_row == height - 1
+    at_edge = home_at == across - 1
+    fraction_y = parts[1] + 0.5
+    fraction_x = parts[0] + 0.5
+
+    def at(rows, mask):
+        return jnp.sum(jnp.where(mask, rows, 0.0), axis=1, keepdims=True)
+
+    inside = []
+    for component in range(2):
+        both = chosen(pick[:, :height], flow[component, pl.ds(THIN, height), wide])
+        inside.append(
+            [
+                at(both[low : low + total], mask)
+                for mask in (this_column, next_column)
+                for low in (0, total)
+            ]
+        )
+
+    def early(i, carry):
+        row = pl.multiple_of(i * 8, 8)
+        rows = pl.ds(row + DEEP - THIN, 8)
+        f1[rows, wide] = row_term(f0, row + DEEP - THIN, wide, flow[1, pl.ds(row, 8), wide])
+        return carry
+
+    lax.fori_loop(2, height // 8, early, 0)
+
+    for copy in halo[:2] + halo[4:]:
         copy.wait()
 
     spot = lax.broadcasted_iota(jnp.int32, (height + 2 * DEEP, LANES), 1)
@@ -279,26 +315,19 @@
         spot < 64, pltpu.roll(after, LANES - 32, 1), pltpu.roll(before, 32, 1)
     )
 
-    column = lax.broadcasted_iota(jnp.int32, (total, width), 1)
-    this_column = column == home_at
-    next_column = column == home_at + 1
-
-    fraction_y = parts[1] + 0.5
-    fraction_x = parts[0] + 0.5
-
     def mixture(component):
-        cells = flow[component, pl.ds(THIN, height + THIN), :]
-        both = chosen(pick, cells)
-        this_row, next_row = both[:total], both[total:]
-
-        def at(rows, mask):
-            return jnp.sum(jnp.where(mask, rows, 0.0), axis=1, keepdims=True)
-
+        low_low, high_low, low_high, high_high = inside[component]
+        below = flow[component, pl.ds(THIN + height, THIN), wide][0:1]
+        beyond = chosen(pick, flow[component, pl.ds(THIN, height + THIN), end])[:, 0:1]
+        high_low = high_low + jnp.where(at_last, at(below, this_column), 0.0)
+        high_high = high_high + jnp.where(at_last, at(below, next_column), 0.0)
+        low_high = low_high + jnp.where(at_edge, beyond[:total], 0.0)
+        high_high = high_high + jnp.where(at_edge, beyond[total:], 0.0)
         return (
-            (1.0 - fraction_y) * (1.0 - fraction_x) * at(this_row, this_column)
-            + fraction_y * (1.0 - fraction_x) * at(next_row, this_column)
-            + (1.0 - fraction_y) * fraction_x * at(this_row, next_column)
-            + fraction_y * fraction_x * at(next_row, next_column)
+            (1.0 - fraction_y) * (1.0 - fraction_x) * low_low
+            + fraction_y * (1.0 - fraction_x) * high_low
+            + (1.0 - fraction_y) * fraction_x * low_high
+            + fraction_y * fraction_x * high_high
         )
 
     new_x = parts[0] + STEP * mixture(0)
@@ -384,7 +413,7 @@
     for copy in own:
         copy.start()
 
-    for copy in halo[-2:]:
+    for copy in halo[2:4]:
         copy.wait()
 
     def first(i, carry):
@@ -395,7 +424,20 @@
         f1[pl.ds(row + DEEP - THIN, 8), :] = here + STEP * term
         return carry
 
-    lax.fori_loop(0, (height + 2 * THIN) // 8, first, 0)
+    def first_inner(i, carry):
+        row = pl.multiple_of(i * 8, 8)
+        rows = pl.ds(row + DEEP - THIN, 8)
+        here = f0[rows, :]
+        along_x = column_term(here, flow[0, pl.ds(row, 8), :])
+        end_y = row_term(f0, row + DEEP - THIN, end, flow[1, pl.ds(row, 8), end])
+        along_y = jnp.concatenate([f1[rows, wide], end_y], axis=1)
+        f1[rows, :] = here - STEP * (along_x + along_y)
+        return carry
+
+    chunks = (height + 2 * THIN) // 8
+    lax.fori_loop(0, 2, first, 0)
+    lax.fori_loop(2, chunks - 2, first_inner, 0)
+    lax.fori_loop(chunks - 2, chunks, first, 0)
 
     def second(i, carry):
         row = pl.multiple_of(i * 8, 8)

time: 21.7 us -> 21.8 us (level)
  no operation moved by 1% of the time
where the time goes in v4:
time: 21.8 us; the launch traced here: 21.5 us
  Pallas kernels  18.9 us (87%)
  local copies, waits for them, and re-layouts  1.31 us (6%)
  between operations  1.29 us (6%)
    pallas_call x1, Pallas kernels, shards(): pl.pallas_call(functools.partial(kernel, nb, nx), out_shape=(pltpu.VMEM((...  18.9 us
    unnamed x2, local copies, waits for them, and re-layouts  1.31 us

profile of v4, /device:TPU:0, one launch (start us, length us, event | category | flops | bytes accessed | tf_op | source)
XLA Modules:
  0.0 21.5 jit_solution(13487049853223668705)
XLA Ops:
  1.3 18.9 %shard_map.95 = (f32[64,512]{1,0:T(8,128)S(1)}, f32[256,128]{1,0:T(8,128)S(1)}) custom-call(f32[64,512]{1,0:T(8,128)} %level_hbm.1, f32[2,64,512]{2,1,0:T(8,128)} %flow_hbm.1, f32[3,64,128]{2,1,0:T(8,128)} %bitcast.3, s32[64,128]{1,0:T(8,128)} %escaped_hbm.1, s32[64]{0:T(128)} %home_hbm.1, s32[64]{0:T(128)} %land_hbm.1, s32[64]{0:T(128)} %dest_hbm.1, ...), custom_call_target="tpu_custom_call" | custom-call | tf_op jit(solution)/shard_map/pallas_call | solution.py:525
  20.2 0.7 %copy.12 = f32[64,512]{1,0:T(8,128)} copy(f32[64,512]{1,0:T(8,128)S(1)} %get-tuple-element.6) | data formatting | bytes 262144
  20.9 0.7 %copy.13 = f32[64,4,128]{2,1,0:T(4,128)} copy(f32[64,4,128]{2,1,0:T(4,128)S(1)} %bitcast.2) | data formatting | bytes 262144

commit v5 on v4

--- a/solution.py
+++ b/solution.py
@@ -511,6 +511,17 @@
         return carry
 
     lax.fori_loop(1, nb, finish_pay, 0)
+
+
+def settle(level_ref, moved_ref, level_hbm, moved_hbm, sem):
+    copies = [
+        pltpu.make_async_copy(level_ref, level_hbm, sem.at[0]),
+        pltpu.make_async_copy(moved_ref, moved_hbm, sem.at[1]),
+    ]
+    for copy in copies:
+        copy.start()
+    for copy in copies:
+        copy.wait()
 
 
 def shards(nb, nx, level_set, velocity, particles, escaped, home, land, dest, count):
@@ -570,6 +581,19 @@
         dest,
         count,
     )
+    level, moved = pl.pallas_call(
+        settle,
+        out_shape=(
+            jax.ShapeDtypeStruct((height, across), f32),
+            jax.ShapeDtypeStruct((rows, per_block), f32),
+        ),
+        in_specs=[vmem, vmem],
+        out_specs=(pl.BlockSpec(memory_space=pl.ANY),) * 2,
+        scratch_shapes=[dma((2,))],
+    )(
+        pltpu.with_memory_space_constraint(level, pltpu.VMEM),
+        pltpu.with_memory_space_constraint(moved, pltpu.VMEM),
+    )
     return level, moved.reshape(nb * CAP, FIELDS, per_block)
 
 

time: 21.8 us -> 21.2 us (0.972)
  local copies, waits for them, and re-layouts: 1.31 us -> 0 us
  Pallas kernels: 18.9 us -> 19.6 us
    unnamed x2 -> x0, local copies, waits for them, and re-layouts: 1.31 us -> none
    pallas_call x0 -> x1, Pallas kernels: none -> 0.72 us  [shards(): pl.pallas_call(settle, out_shape=(jax.ShapeDtypeStruct((height, across),...]
where the time goes in v5:
time: 21.2 us; the launch traced here: 20.9 us
  Pallas kernels  19.6 us (92%)
  between operations  1.29 us (6%)
    pallas_call x1, Pallas kernels, shards(): pl.pallas_call(functools.partial(kernel, nb, nx), out_shape=(pltpu.VMEM((...  18.9 us
    pallas_call x1, Pallas kernels, shards(): pl.pallas_call(settle, out_shape=(jax.ShapeDtypeStruct((height, across),...  0.72 us

profile of v5, /device:TPU:0, one launch (start us, length us, event | category | flops | bytes accessed | tf_op | source)
XLA Modules:
  0.0 20.9 jit_solution(11067544990557981082)
XLA Ops:
  1.3 18.9 %shard_map.95 = (f32[64,512]{1,0:T(8,128)S(1)}, f32[256,128]{1,0:T(8,128)S(1)}) custom-call(f32[64,512]{1,0:T(8,128)} %level_hbm.1, f32[2,64,512]{2,1,0:T(8,128)} %flow_hbm.1, f32[3,64,128]{2,1,0:T(8,128)} %bitcast.2, s32[64,128]{1,0:T(8,128)} %escaped_hbm.1, s32[64]{0:T(128)} %home_hbm.1, s32[64]{0:T(128)} %land_hbm.1, s32[64]{0:T(128)} %dest_hbm.1, ...), custom_call_target="tpu_custom_call" | custom-call | tf_op jit(solution)/shard_map/pallas_call | solution.py:536
  20.2 0.7 %shard_map.96 = (f32[64,512]{1,0:T(8,128)}, f32[256,128]{1,0:T(8,128)}) custom-call(f32[64,512]{1,0:T(8,128)S(1)} %get-tuple-element.6.level_ref, f32[256,128]{1,0:T(8,128)S(1)} %get-tuple-element.7.moved_ref), custom_call_target="tpu_custom_call" | custom-call | tf_op jit(solution)/shard_map/pallas_call | solution.py:584

commit v6 on v5

--- a/solution.py
+++ b/solution.py
@@ -337,31 +337,6 @@
     for k in range(FIELDS):
         packed[pl.ds(k, nb * CAP, stride=FIELDS), :] = payload[:, k * LANES : (k + 1) * LANES]
 
-    gy = new_y + 0.5
-    gx = new_x + 0.5
-
-    def over(rows):
-        return jnp.sum(rows, axis=1, keepdims=True)
-
-    columns = (
-        land_row.astype(jnp.float32),
-        (land_col - land_row * across).astype(jnp.float32),
-        over(weight * (1.0 - gy) * (1.0 - gx)),
-        over(weight * gy * (1.0 - gx)),
-        over(weight * (1.0 - gy) * gx),
-        over(weight * gy * gx),
-    )
-    spot = lax.broadcasted_iota(jnp.int32, (total, LANES), 1)
-    table = jnp.zeros((total, LANES), jnp.float32)
-    for k, one in enumerate(columns):
-        table = jnp.where(spot // (2 * CAP) == k, one, table)
-    place = spot % (2 * CAP)
-    sheet = chosen(own_hot, jnp.where(place == rank_col, table, 0.0)) + chosen(
-        past_hot, jnp.where(place == rank_col + CAP, table, 0.0)
-    )
-    for band in range(nb):
-        records[band] = sheet[band : band + 1]
-
     per = CAP * FIELDS
     mine = pl.ds(pl.multiple_of(g * per, per), per)
 
@@ -399,13 +374,43 @@
         )
 
     def start_far(k, carry):
+        pay_copy(k).start()
+        return carry
+
+    def start_records(k, carry):
         rec_copy(k).start()
         left_copy(k).start()
-        pay_copy(k).start()
-        return carry
+        return carry
+
+    lax.fori_loop(1, nb, start_far, 0)
+
+    gy = new_y + 0.5
+    gx = new_x + 0.5
+
+    def over(rows):
+        return jnp.sum(rows, axis=1, keepdims=True)
+
+    columns = (
+        land_row.astype(jnp.float32),
+        (land_col - land_row * across).astype(jnp.float32),
+        over(weight * (1.0 - gy) * (1.0 - gx)),
+        over(weight * gy * (1.0 - gx)),
+        over(weight * (1.0 - gy) * gx),
+        over(weight * gy * gx),
+    )
+    spot = lax.broadcasted_iota(jnp.int32, (total, LANES), 1)
+    table = jnp.zeros((total, LANES), jnp.float32)
+    for k, one in enumerate(columns):
+        table = jnp.where(spot // (2 * CAP) == k, one, table)
+    place = spot % (2 * CAP)
+    sheet = chosen(own_hot, jnp.where(place == rank_col, table, 0.0)) + chosen(
+        past_hot, jnp.where(place == rank_col + CAP, table, 0.0)
+    )
+    for band in range(nb):
+        records[band] = sheet[band : band + 1]
 
     left_copy(0).start()
-    lax.fori_loop(1, nb, start_far, 0)
+    lax.fori_loop(1, nb, start_records, 0)
     own = [
         pltpu.make_async_copy(packed.at[mine], moved_hbm.at[mine], own_sem.at[0]),
         pltpu.make_async_copy(records.at[g], rec_same.at[g], own_sem.at[1]),

time: 21.2 us -> 21.9 us (1.033)
  Pallas kernels: 19.6 us -> 20.4 us
    pallas_call x1, Pallas kernels: 18.9 us -> 19.7 us  [shards(): pl.pallas_call(functools.partial(kernel, nb, nx), out_shape=(pltpu.VMEM((...]
where the time goes in v6:
time: 21.9 us; the launch traced here: 21.7 us
  Pallas kernels  20.4 us (93%)
  between operations  1.29 us (6%)
    pallas_call x1, Pallas kernels, shards(): pl.pallas_call(functools.partial(kernel, nb, nx), out_shape=(pltpu.VMEM((...  19.7 us
    pallas_call x1, Pallas kernels, shards(): pl.pallas_call(settle, out_shape=(jax.ShapeDtypeStruct((height, across),...  0.72 us

profile of v6, /device:TPU:0, one launch (start us, length us, event | category | flops | bytes accessed | tf_op | source)
XLA Modules:
  0.0 21.7 jit_solution(3167403319828772531)
XLA Ops:
  1.3 19.7 %shard_map.95 = (f32[64,512]{1,0:T(8,128)S(1)}, f32[256,128]{1,0:T(8,128)S(1)}) custom-call(f32[64,512]{1,0:T(8,128)} %level_hbm.1, f32[2,64,512]{2,1,0:T(8,128)} %flow_hbm.1, f32[3,64,128]{2,1,0:T(8,128)} %bitcast.2, s32[64,128]{1,0:T(8,128)} %escaped_hbm.1, s32[64]{0:T(128)} %home_hbm.1, s32[64]{0:T(128)} %land_hbm.1, s32[64]{0:T(128)} %dest_hbm.1, ...), custom_call_target="tpu_custom_call" | custom-call | tf_op jit(solution)/shard_map/pallas_call | solution.py:541
  21.0 0.7 %shard_map.96 = (f32[64,512]{1,0:T(8,128)}, f32[256,128]{1,0:T(8,128)}) custom-call(f32[64,512]{1,0:T(8,128)S(1)} %get-tuple-element.6.level_ref, f32[256,128]{1,0:T(8,128)S(1)} %get-tuple-element.7.moved_ref), custom_call_target="tpu_custom_call" | custom-call | tf_op jit(solution)/shard_map/pallas_call | solution.py:589
